TPU v7x, 128 devices: a whole 4x4x4 slice. The times are simulated.
128 devices in a mesh: row: 16 (over x, z), col: 8 (over y, core).
Axes of the slice: x: 4, y: 4, z: 4, core: 2. Of those that a mesh axis runs over, the one named last changes fastest.
Arguments:
- tokens: bfloat16 [384, 8192], P('col', 'row'), may hold values from -6 to 6
- gate_weight: bfloat16 [8192, 26624], P('row', 'col'), may hold values from -0.09375 to 0.09375
- up_weight: bfloat16 [8192, 26624], P('row', 'col'), may hold values from -0.09375 to 0.09375
- down_weight: bfloat16 [26624, 8192], P('col', 'row'), may hold values from -0.0546875 to 0.0546875
- gate_mask: int32 [64, 208], P('row', 'col'), may hold values from 0 to 1, as said below
- up_mask: int32 [64, 208], P('row', 'col'), may hold values from 0 to 1, as said below
- down_mask: int32 [208, 64], P('col', 'row'), may hold values from 0 to 1, as said below
- out_grad: bfloat16 [384, 8192], P('col', 'row'), may hold values from -6 to 6
Outputs:
- mixed_out: bfloat16 [384, 8192], P('col', 'row')
- grad_gate: bfloat16 [8192, 26624], P('row', 'col')
- grad_up: bfloat16 [8192, 26624], P('row', 'col')
- grad_down: bfloat16 [26624, 8192], P('col', 'row')
- input_grad: bfloat16 [384, 8192], P('col', 'row')
Inputs may be any that keep to these rules, and one draw needn't show every extreme that they name: `gate_mask`: 1 keeps a tile of 128 x 128 weights, 0 drops it; the share kept differs between rows of tiles. `up_mask`: 1 keeps a tile of 128 x 128 weights, 0 drops it; the share kept differs between rows of tiles. `down_mask`: 1 keeps a tile of 128 x 128 weights, 0 drops it; the share kept differs between columns of tiles.
All inputs are finite; a program needn't handle non-finite values.
Results may differ from a plain program's by a relative error of at most 0.0049.
Values may be sent and summed in bfloat16 or wider, within the bound.
A program may use at most 128 MiB of HBM per device.

v0:
```python
import jax
import jax.numpy as jnp
from jax import lax
from jax.sharding import PartitionSpec as P


def expand(weight, mask):
    rows_w, cols_w = weight.shape
    tile_size = rows_w // mask.shape[0]
    blocks = weight.reshape(mask.shape[0], tile_size, mask.shape[1], tile_size)
    kept = mask.astype(weight.dtype)[:, None, :, None]
    return (blocks * kept).reshape(rows_w, cols_w)


def contract_last(left, right):
    return lax.dot_general(
        left, right, (((1,), (1,)), ((), ())), preferred_element_type=jnp.float32
    )


def contract_first(left, right):
    return lax.dot_general(
        left, right, (((0,), (0,)), ((), ())), preferred_element_type=jnp.float32
    )


def body(tokens, gate_weight, up_weight, down_weight, gate_mask, up_mask, down_mask, out_grad):
    feat = tokens.shape[1]
    both_all = lax.all_gather(
        jnp.concatenate([tokens, out_grad], axis=1), "col", axis=0, tiled=True
    )
    tok_all = both_all[:, :feat]
    grad_all = both_all[:, feat:]
    w_gate = expand(gate_weight, gate_mask)
    w_up = expand(up_weight, up_mask)
    w_down = expand(down_weight, down_mask)
    gate_mine = lax.psum_scatter(
        jnp.dot(tok_all, w_gate, preferred_element_type=jnp.float32),
        "row",
        scatter_dimension=0,
        tiled=True,
    )
    up_mine = lax.psum_scatter(
        jnp.dot(tok_all, w_up, preferred_element_type=jnp.float32),
        "row",
        scatter_dimension=0,
        tiled=True,
    )
    sigmoid_gate = jax.nn.sigmoid(gate_mine)
    silu_gate = gate_mine * sigmoid_gate
    hidden_mine = (silu_gate * up_mine).astype(jnp.bfloat16)
    hidden_all = lax.all_gather(hidden_mine, "row", axis=0, tiled=True)
    hidden_grad = lax.psum_scatter(
        contract_last(grad_all, w_down), "row", scatter_dimension=0, tiled=True
    )
    gate_grad = (
        hidden_grad * up_mine * sigmoid_gate * (1.0 + gate_mine * (1.0 - sigmoid_gate))
    ).astype(jnp.bfloat16)
    up_grad = (hidden_grad * silu_gate).astype(jnp.bfloat16)
    grad_pair = lax.all_gather(
        jnp.concatenate([gate_grad, up_grad], axis=1), "row", axis=0, tiled=True
    )
    half_width = gate_weight.shape[1]
    weight_pair = contract_first(tok_all, grad_pair)
    grad_gate = expand(weight_pair[:, :half_width], gate_mask).astype(jnp.bfloat16)
    grad_up = expand(weight_pair[:, half_width:], up_mask).astype(jnp.bfloat16)
    grad_down = expand(contract_first(hidden_all, grad_all), down_mask).astype(jnp.bfloat16)
    mixed_part = jnp.dot(hidden_all, w_down, preferred_element_type=jnp.float32)
    input_part = contract_last(grad_pair[:, :half_width], w_gate) + contract_last(
        grad_pair[:, half_width:], w_up
    )
    out_sums = lax.psum_scatter(
        jnp.concatenate([mixed_part, input_part], axis=1), "col", scatter_dimension=0, tiled=True
    )
    mixed_out = out_sums[:, :feat].astype(jnp.bfloat16)
    input_grad = out_sums[:, feat:].astype(jnp.bfloat16)
    return (mixed_out, grad_gate, grad_up, grad_down, input_grad)


def solution(mesh):
    in_specs = (
        P("col", "row"),
        P("row", "col"),
        P("row", "col"),
        P("col", "row"),
        P("row", "col"),
        P("row", "col"),
        P("col", "row"),
        P("col", "row"),
    )
    out_specs = (
        P("col", "row"),
        P("row", "col"),
        P("row", "col"),
        P("col", "row"),
        P("col", "row"),
    )
    return jax.shard_map(body, mesh=mesh, in_specs=in_specs, out_specs=out_specs, check_vma=False)
```

profile of v0, /device:TPU:1, one launch (start us, length us, event | category | flops | bytes accessed | tf_op | source)
XLA Modules:
  0.0 446.2 jit_solution(16238817399744067588)
XLA Ops:
  8.0 16.3 %all_gather.9 = bf16[384,1024]{1,0:T(8,128)(2,1)} all-gather(bf16[48,1024]{1,0:T(8,128)(2,1)S(1)} %pad_maximum_fusion.2), channel_id=1, replica_groups=mesh['row'=16,'col'=8] {'col'}, dimensions={0}, use_global_device_ids=true | all-gather | bytes 884736 | tf_op jit(solution)/shard_map/all_gather | solution.py:29
  25.2 4.2 copy.26
  29.5 0.9 mul.87
  30.4 1.7 copy-done
  32.2 3.9 fusion.10
  36.8 5.6 %copy.28 = bf16[512,3328]{0,1:T(8,128)(2,1)} copy(bf16[512,3328]{1,0:T(8,128)(2,1)} %param.10) | data formatting | bytes 6815744 | tf_op args[2]
  42.4 0.9 mul.91
  43.4 1.7 copy-done.3
  45.1 4.9 %fusion.11 = f32[384,3328]{1,0:T(8,128)} fusion(bf16[512,3328]{0,1:T(8,128)(2,1)S(1)} %copy-done.2, bf16[416,8,4,128]{3,2,1,0:T(4,128)(2,1)S(1)} %bitcast.53, bf16[384,1024]{1,0:T(8,128)(2,1)} %all_gather.9), kind=kOutput, calls=%fused_computation.18 | convolution fusion | flops 1310326784 | bytes 12320768 | tf_op jit(solution)/shard_map/dot_general | solution.py:44
  50.8 0.9 mul.95
  51.8 1.7 copy-done.4
  53.5 5.9 %fusion.12 = f32[384,3328]{1,0:T(8,128)} fusion(bf16[3328,512]{1,0:T(8,128)(2,1)} %param.11, bf16[416,8,4,128]{3,2,1,0:T(4,128)(2,1)S(1)} %bitcast.55, bf16[384,1024]{1,0:T(8,128)(2,1)S(1)} %copy-done.6), kind=kOutput, calls=%fused_computation.19 | convolution fusion | flops 1310326784 | bytes 12320768 | tf_op jit(solution)/shard_map/dot_general | solution.py:16
  59.4 56.1 %reduce-scatter.13.cloned.1.call-done = f32[24,3328]{1,0:T(8,128)} async-done(((f32[384,3328]{1,0:T(8,128)}), f32[24,3328]{1,0:T(8,128)}) %reduce-scatter.13.cloned.1.call-update) | async-done | bytes 319504
  115.5 82.6 %reduce-scatter.15.cloned.1.call-done = f32[24,3328]{1,0:T(8,128)} async-done(((f32[384,3328]{1,0:T(8,128)}), f32[24,3328]{1,0:T(8,128)}) %reduce-scatter.15.cloned.1.call-update) | async-done | bytes 319504
  198.1 82.6 %reduce-scatter.17.cloned.1.call-done = f32[24,3328]{1,0:T(8,128)} async-done(((f32[384,3328]{1,0:T(8,128)}), f32[24,3328]{1,0:T(8,128)}) %reduce-scatter.17.cloned.1.call-update) | async-done | bytes 319504
  280.7 2.1 multiply_convert_fusion.2
  282.9 1.8 pad_maximum_fusion.1
  284.9 44.2 %all-gather.3.cloned.1.call-done = bf16[384,3328]{1,0:T(8,128)(2,1)} async-done(((bf16[24,3328]{1,0:T(8,128)(2,1)}), bf16[384,3328]{1,0:T(8,128)(2,1)}) %all-gather.3.cloned.1.call-update) | async-done | bytes 2555920 | tf_op jit(solution)/shard_map/all_gather | solution.py:52
  329.1 6.1 %fusion.13 = f32[384,512]{1,0:T(8,128)} fusion(bf16[384,3328]{1,0:T(8,128)(2,1)} %all-gather.3.cloned.1.call-done, bf16[3328,512]{1,0:T(8,128)(2,1)} %param.11, bf16[416,8,4,128]{3,2,1,0:T(4,128)(2,1)} %bitcast.56), kind=kOutput, calls=%fused_computation.20 | convolution fusion | flops 1310326784 | bytes 10158080 | tf_op jit(solution)/shard_map/dot_general | solution.py:68
  335.2 51.6 %all-gather.5.cloned.1.call-done = bf16[384,6656]{1,0:T(8,128)(2,1)} async-done(((bf16[24,6656]{1,0:T(8,128)(2,1)}), bf16[384,6656]{1,0:T(8,128)(2,1)}) %all-gather.5.cloned.1.call-update) | async-done | bytes 5111824 | tf_op jit(solution)/shard_map/all_gather | solution.py:60
  386.8 5.4 %fusion.3 = f32[384,512]{1,0:T(8,128)S(1)} fusion(bf16[384,6656]{1,0:T(8,128)(2,1)} %all-gather.5.cloned.1.call-done, bf16[512,3328]{0,1:T(8,128)(2,1)} %copy.28, bf16[416,8,4,128]{3,2,1,0:T(4,128)(2,1)} %bitcast.54), kind=kOutput, calls=%fused_computation.11 | convolution fusion | flops 1310326784 | bytes 10158080 | tf_op jit(solution)/shard_map/dot_general | solution.py:16
  393.0 1.5 fusion.7
  394.5 1.4 pad_maximum_fusion
  396.0 0.9 mul.103
  397.0 3.6 copy.54
  400.6 7.7 %copy.31 = f32[512,3328]{1,0:T(8,128)} copy(f32[512,3328]{0,1:T(8,128)} %bitcast.48) | data formatting | bytes 13631488 | tf_op jit(solution)/shard_map/mul | solution.py:12
  408.4 0.9 mul.106
  409.3 3.5 copy.53
  412.8 7.7 %copy.33 = f32[512,3328]{1,0:T(8,128)} copy(f32[512,3328]{0,1:T(8,128)} %bitcast.50) | data formatting | bytes 13631488 | tf_op jit(solution)/shard_map/mul | solution.py:12
  422.6 3.8 fusion
  426.3 3.8 fusion.17
  430.1 7.7 %fusion.1 = (bf16[512,3328]{1,0:T(8,128)(2,1)}, bf16[512,3328]{1,0:T(8,128)(2,1)}) fusion(f32[512,3328]{1,0:T(8,128)} %copy.33, f32[512,6656]{1,0:T(8,128)S(1)} %fusion.17, f32[512,3328]{1,0:T(8,128)} %copy.31), kind=kLoop, calls=%fused_computation.5 | loop fusion | flops 6815744 | bytes 34078720 | tf_op jit(solution)/shard_map/convert_element_type | solution.py:66
  (54 shorter events, 8.4 us)
Async XLA Ops:
  7.2 108.3 %reduce-scatter.13.cloned.1.call-start = ((), (), s32[]{:S(2)}) async-start(), calls=%async_computation.7 | async-start | bytes 5431296
  29.5 2.7 copy-start.5
  30.4 1.8 copy-start
  36.0 0.7 copy-start.11
  36.1 162.0 %reduce-scatter.15.cloned.1.call-start = ((), (), s32[]{:S(2)}) async-start(), calls=%async_computation.8 | async-start | bytes 5431296
  42.4 2.7 copy-start.2
  43.4 1.8 copy-start.3
  50.0 0.7 copy-start.12
  50.0 230.7 %reduce-scatter.17.cloned.1.call-start = ((), (), s32[]{:S(2)}) async-start(), calls=%async_computation.9 | async-start | bytes 5431296
  50.8 2.7 copy-start.6
  51.7 1.7 copy-start.4
  59.4 269.7 %all-gather.3.cloned.1.call-start = ((), (), s32[]{:S(2)}) async-start(), calls=%async_computation.4 | async-start | bytes 2715648 | tf_op jit(solution)/shard_map/all_gather | solution.py:52
  282.8 104.0 %all-gather.5.cloned.1.call-start = ((), (), s32[]{:S(2)}) async-start(), calls=%async_computation.5 | async-start | bytes 5431296 | tf_op jit(solution)/shard_map/all_gather | solution.py:60
  284.7 153.1 %reduce-scatter.11.cloned.1.call-start = ((), (), s32[]{:S(2)}) async-start(), calls=%async_computation.6 | async-start | bytes 1769472 | tf_op jit(solution)/shard_map/reduce_scatter | solution.py:72
  386.8 5.4 %copy-start.1 = (bf16[4,128,26,128]{1,0,3,2:T(4,128)(2,1)S(1)}, bf16[4,128,26,128]{1,0,3,2:T(4,128)(2,1)}, u32[]{:S(2)}) copy-start(bf16[4,128,26,128]{1,0,3,2:T(4,128)(2,1)} %copy-done) | copy-start | bytes 10223620
  386.8 6.2 %copy-start.9 = (bf16[384,6656]{1,0:T(8,128)(2,1)S(1)}, bf16[384,6656]{1,0:T(8,128)(2,1)}, u32[]{:S(2)}) copy-start(bf16[384,6656]{1,0:T(8,128)(2,1)} %all-gather.5.cloned.1.call-done) | copy-start | bytes 15335428
  393.0 1.5 copy-start.10
  420.6 1.1 copy-start.7
  420.6 2.0 copy-start.8
  420.6 5.7 %slice-start = ((s8[5111808]{0:T(1024)(128)(4,1)}), s8[4194304]{0:T(1024)(128)(4,1)S(1)}, s32[]{:S(2)}) async-start(s8[5111808]{0:T(1024)(128)(4,1)} %bitcast.57), calls=%async_computation.10 | async-start | bytes 8388608
  422.6 3.8 slice-start.1
Sparse Core Ops, SparseCore 0:
  36.2 79.2 reduce-scatter.12
  118.9 79.1 reduce-scatter.14
  201.4 79.1 reduce-scatter.16
  282.9 46.0 all-gather.2
  331.1 55.6 all-gather.4
  396.1 29.9 reduce-scatter.10
where the time goes:
time: 447 us; the launch traced here: 446 us
  waiting for transfers between devices  317 us (71%)
  local copies, waits for them, and re-layouts  47.5 us (11%)
  matrix products  35.1 us (8%)
  blocking collectives  16.3 us (4%)
  other arithmetic  15.5 us (3%)
  between operations  14.3 us (3%)
    unnamed x9, waiting for transfers between devices  221 us
    all_gather x1, waiting for transfers between devices, body(): lax.all_gather(jnp.concatenate([gate_grad, up_grad], axis=1), 'row', axis...  51.6 us
    all_gather x1, waiting for transfers between devices, body(): hidden_all = lax.all_gather(hidden_mine, 'row', axis=0, tiled=True)  44.2 us
    unnamed x34, local copies, waits for them, and re-layouts  25.3 us
    mul x8, local copies, waits for them, and re-layouts, expand(): return (blocks * kept).reshape(rows_w, cols_w)  21 us
    all_gather x1, blocking collectives, body(): lax.all_gather(jnp.concatenate([tokens, out_grad], axis=1), 'col', axis=0...  16.3 us
    dot_general x3, matrix products, contract_last(): lax.dot_general(left, right, (((1,), (1,)), ((), ())), preferred_element_...  12.7 us
  transfers between devices with their start and end apart: 6, of which 5 were waited for; matrix products, arithmetic and copies ran while one was open for 15% of the time, Pallas kernels for 0%

commit v1 on v0

--- a/solution.py
+++ b/solution.py
@@ -2,6 +2,27 @@
 import jax.numpy as jnp
 from jax import lax
 from jax.sharding import PartitionSpec as P
+
+
+def collect(value, axis, dim):
+    peers, position, extent = (lax.axis_size(axis), lax.axis_index(axis), value.shape[dim])
+    upward = [(i, (i + 1) % peers) for i in range(peers)]
+    left = [(i, (i - 1) % peers) for i in range(peers)]
+    whole = jnp.zeros((*value.shape[:dim], peers * extent, *value.shape[dim + 1 :]), value.dtype)
+    whole = lax.dynamic_update_slice_in_dim(whole, value, position * extent, axis=dim)
+    from_left = from_right = value
+    half = peers // 2
+    for step in range(1, half + 1):
+        from_left = lax.ppermute(from_left, axis, upward)
+        whole = lax.dynamic_update_slice_in_dim(
+            whole, from_left, (position - step) % peers * extent, axis=dim
+        )
+        if step < peers - half:
+            from_right = lax.ppermute(from_right, axis, left)
+            whole = lax.dynamic_update_slice_in_dim(
+                whole, from_right, (position + step) % peers * extent, axis=dim
+            )
+    return whole
 
 
 def expand(weight, mask):
@@ -49,7 +70,7 @@
     sigmoid_gate = jax.nn.sigmoid(gate_mine)
     silu_gate = gate_mine * sigmoid_gate
     hidden_mine = (silu_gate * up_mine).astype(jnp.bfloat16)
-    hidden_all = lax.all_gather(hidden_mine, "row", axis=0, tiled=True)
+    hidden_all = collect(hidden_mine, "row", 0)
     hidden_grad = lax.psum_scatter(
         contract_last(grad_all, w_down), "row", scatter_dimension=0, tiled=True
     )

time: 447 us -> 430 us (0.962)
  the two profiles are of different devices: /device:TPU:1 before, /device:TPU:0 now
where the time goes in v1:
time: 430 us
  waiting for transfers between devices  272 us (63%)
  local copies, waits for them, and re-layouts  46.4 us (11%)
  starting transfers between devices  38.9 us (9%)
  matrix products  31.5 us (7%)
  between operations  14.2 us (3%)
  blocking collectives  14 us (3%)
  other arithmetic  12.2 us (3%)
    unnamed x8, waiting for transfers between devices  228 us
    ppermute x7, starting transfers between devices, collect(): from_right = lax.ppermute(from_right, axis, left)  37.5 us
    ppermute x8, waiting for transfers between devices, collect(): from_left = lax.ppermute(from_left, axis, upward)  37.1 us
    unnamed x46, local copies, waits for them, and re-layouts  23.6 us
    mul x8, local copies, waits for them, and re-layouts, expand(): return (blocks * kept).reshape(rows_w, cols_w)  21.2 us
    all_gather x1, blocking collectives, body(): lax.all_gather(jnp.concatenate([tokens, out_grad], axis=1), 'col', axis=0...  14 us
    dot_general x3, matrix products, contract_last(): lax.dot_general(left, right, (((1,), (1,)), ((), ())), preferred_element_...  10.8 us
    dot_general x2, matrix products, contract_first(): lax.dot_general(left, right, (((0,), (0,)), ((), ())), preferred_element_...  9.45 us
  transfers between devices with their start and end apart: 20, of which 13 were waited for; matrix products, arithmetic and copies ran while one was open for 14% of the time, Pallas kernels for 0%

profile of v1, /device:TPU:0, one launch (start us, length us, event | category | flops | bytes accessed | tf_op | source)
XLA Modules:
  0.0 429.7 jit_solution(16458198252566617165)
XLA Ops:
  7.2 4.3 copy.26
  11.7 14.0 %all_gather.6 = bf16[384,1024]{1,0:T(8,128)(2,1)S(1)} all-gather(bf16[48,1024]{1,0:T(8,128)(2,1)S(1)} %pad_maximum_fusion.2), channel_id=1, replica_groups=mesh['row'=16,'col'=8] {'col'}, dimensions={0}, use_global_device_ids=true | all-gather | bytes 884736 | tf_op jit(solution)/shard_map/all_gather | solution.py:50
  28.4 3.9 fusion.10
  35.8 3.9 fusion.12
  39.8 4.3 %copy.28 = bf16[512,3328]{0,1:T(8,128)(2,1)S(1)} copy(bf16[512,3328]{1,0:T(8,128)(2,1)} %param.10) | data formatting | bytes 6815744 | tf_op args[2]
  47.0 3.9 fusion.11
  50.9 63.2 %reduce-scatter.13.cloned.1.call-done = f32[24,3328]{1,0:T(8,128)} async-done(((f32[384,3328]{1,0:T(8,128)}), f32[24,3328]{1,0:T(8,128)}) %reduce-scatter.13.cloned.1.call-update) | async-done | bytes 319504
  114.1 82.6 %reduce-scatter.17.cloned.1.call-done = f32[24,3328]{1,0:T(8,128)} async-done(((f32[384,3328]{1,0:T(8,128)}), f32[24,3328]{1,0:T(8,128)}) %reduce-scatter.17.cloned.1.call-update) | async-done | bytes 319504
  196.7 82.6 %reduce-scatter.15.cloned.1.call-done = f32[24,3328]{1,0:T(8,128)} async-done(((f32[384,3328]{1,0:T(8,128)}), f32[24,3328]{1,0:T(8,128)}) %reduce-scatter.15.cloned.1.call-update) | async-done | bytes 319504
  283.0 4.3 collective-permute-start.1
  290.5 5.3 %collective-permute-start.3 = (bf16[24,3328]{1,0:T(8,128)(2,1)S(1)}, bf16[24,3328]{1,0:T(8,128)(2,1)S(1)}, u32[]{:S(2)}, u32[]{:S(2)}) collective-permute-start(bf16[24,3328]{1,0:T(8,128)(2,1)S(1)} %collective-permute-done.1), channel_id=1, source_target_pairs={{0,120},{8,0},{16,8},{24,16},{32,24},{40,32},{48,40},{56,48},{64,5... | collective-permute-start | bytes 479240 | tf_op jit(solution)/shard_map/ppermute | solution.py:21
  295.9 6.1 %collective-permute-done.2 = bf16[24,3328]{1,0:T(8,128)(2,1)S(1)} collective-permute-done((bf16[24,3328]{1,0:T(8,128)(2,1)S(1)}, bf16[24,3328]{1,0:T(8,128)(2,1)S(1)}, u32[]{:S(2)}, u32[]{:S(2)}) %collective-permute-start.2) | collective-permute-done | bytes 159776 | tf_op jit(solution)/shard_map/ppermute | solution.py:16
  301.9 5.3 %collective-permute-start.5 = (bf16[24,3328]{1,0:T(8,128)(2,1)S(1)}, bf16[24,3328]{1,0:T(8,128)(2,1)S(1)}, u32[]{:S(2)}, u32[]{:S(2)}) collective-permute-start(bf16[24,3328]{1,0:T(8,128)(2,1)S(1)} %collective-permute-done.3), channel_id=1, source_target_pairs={{0,120},{8,0},{16,8},{24,16},{32,24},{40,32},{48,40},{56,48},{64,5... | collective-permute-start | bytes 479240 | tf_op jit(solution)/shard_map/ppermute | solution.py:21
  307.3 3.5 collective-permute-done.4
  310.8 5.6 %collective-permute-start.7 = (bf16[24,3328]{1,0:T(8,128)(2,1)S(1)}, bf16[24,3328]{1,0:T(8,128)(2,1)S(1)}, u32[]{:S(2)}, u32[]{:S(2)}) collective-permute-start(bf16[24,3328]{1,0:T(8,128)(2,1)S(1)} %collective-permute-done.5), channel_id=1, source_target_pairs={{0,120},{8,0},{16,8},{24,16},{32,24},{40,32},{48,40},{56,48},{64,5... | collective-permute-start | bytes 479240 | tf_op jit(solution)/shard_map/ppermute | solution.py:21
  316.5 4.4 %collective-permute-done.6 = bf16[24,3328]{1,0:T(8,128)(2,1)S(1)} collective-permute-done((bf16[24,3328]{1,0:T(8,128)(2,1)S(1)}, bf16[24,3328]{1,0:T(8,128)(2,1)S(1)}, u32[]{:S(2)}, u32[]{:S(2)}) %collective-permute-start.6) | collective-permute-done | bytes 159776 | tf_op jit(solution)/shard_map/ppermute | solution.py:16
  320.9 3.4 collective-permute-done.7
  324.3 5.8 %collective-permute-start.9 = (bf16[24,3328]{1,0:T(8,128)(2,1)S(1)}, bf16[24,3328]{1,0:T(8,128)(2,1)S(1)}, u32[]{:S(2)}, u32[]{:S(2)}) collective-permute-start(bf16[24,3328]{1,0:T(8,128)(2,1)S(1)} %collective-permute-done.7), channel_id=1, source_target_pairs={{0,120},{8,0},{16,8},{24,16},{32,24},{40,32},{48,40},{56,48},{64,5... | collective-permute-start | bytes 479240 | tf_op jit(solution)/shard_map/ppermute | solution.py:21
  330.2 4.2 collective-permute-done.8
  337.8 5.8 %collective-permute-start.11 = (bf16[24,3328]{1,0:T(8,128)(2,1)S(1)}, bf16[24,3328]{1,0:T(8,128)(2,1)S(1)}, u32[]{:S(2)}, u32[]{:S(2)}) collective-permute-start(bf16[24,3328]{1,0:T(8,128)(2,1)S(1)} %collective-permute-done.9), channel_id=1, source_target_pairs={{0,120},{8,0},{16,8},{24,16},{32,24},{40,32},{48,40},{56,48},{64,5... | collective-permute-start | bytes 479240 | tf_op jit(solution)/shard_map/ppermute | solution.py:21
  343.6 4.0 collective-permute-done.10
  347.6 5.3 %collective-permute-start.13 = (bf16[24,3328]{1,0:T(8,128)(2,1)S(1)}, bf16[24,3328]{1,0:T(8,128)(2,1)S(1)}, u32[]{:S(2)}, u32[]{:S(2)}) collective-permute-start(bf16[24,3328]{1,0:T(8,128)(2,1)S(1)} %collective-permute-done.11), channel_id=1, source_target_pairs={{0,120},{8,0},{16,8},{24,16},{32,24},{40,32},{48,40},{56,48},{64,5... | collective-permute-start | bytes 479240 | tf_op jit(solution)/shard_map/ppermute | solution.py:21
  356.3 8.5 %collective-permute-done.14 = bf16[24,3328]{1,0:T(8,128)(2,1)S(1)} collective-permute-done((bf16[24,3328]{1,0:T(8,128)(2,1)S(1)}, bf16[24,3328]{1,0:T(8,128)(2,1)S(1)}, u32[]{:S(2)}, u32[]{:S(2)}) %collective-permute-start.14) | collective-permute-done | bytes 159776 | tf_op jit(solution)/shard_map/ppermute | solution.py:16
  364.9 3.5 fusion.13
  368.5 5.4 %fusion.3 = f32[384,512]{1,0:T(8,128)S(1)} fusion(bf16[384,6656]{1,0:T(8,128)(2,1)} %all-gather.2.cloned.1.call-done, bf16[512,3328]{0,1:T(8,128)(2,1)} %copy-done.6, bf16[416,8,4,128]{3,2,1,0:T(4,128)(2,1)} %bitcast.56), kind=kOutput, calls=%fused_computation.11 | convolution fusion | flops 1310326784 | bytes 10158080 | tf_op jit(solution)/shard_map/dot_general | solution.py:37
  379.5 3.6 copy.53
  383.1 7.8 %copy.33 = f32[512,3328]{1,0:T(8,128)} copy(f32[512,3328]{0,1:T(8,128)} %bitcast.48) | data formatting | bytes 13631488 | tf_op jit(solution)/shard_map/mul | solution.py:33
  391.9 3.5 copy.54
  395.4 7.7 %copy.31 = f32[512,3328]{1,0:T(8,128)} copy(f32[512,3328]{0,1:T(8,128)} %bitcast.50) | data formatting | bytes 13631488 | tf_op jit(solution)/shard_map/mul | solution.py:33
  404.4 3.7 fusion
  408.1 5.7 %fusion.17 = f32[512,6656]{1,0:T(8,128)S(1)} fusion(bf16[384,6656]{1,0:T(8,128)(2,1)} %all-gather.2.cloned.1.call-done, bf16[384,1024]{1,0:T(8,128)(2,1)S(1)} %copy-done.11), kind=kOutput, calls=%fused_computation.29 | convolution fusion | flops 2617245696 | bytes 19136512 | tf_op jit(solution)/shard_map/dot_general | solution.py:43
  413.9 7.7 %fusion.1 = (bf16[512,3328]{1,0:T(8,128)(2,1)}, bf16[512,3328]{1,0:T(8,128)(2,1)}) fusion(f32[512,3328]{1,0:T(8,128)} %copy.33, f32[512,6656]{1,0:T(8,128)S(1)} %fusion.17, f32[512,3328]{1,0:T(8,128)} %copy.31), kind=kLoop, calls=%fused_computation.5 | loop fusion | flops 6815744 | bytes 34078720 | tf_op jit(solution)/shard_map/convert_element_type | solution.py:87
  (109 shorter events, 32.5 us)
Async XLA Ops:
  7.2 4.3 %copy-start.18 = (s32[4,26]{1,0:T(4,128)S(1)}, s32[4,26]{1,0:T(4,128)}, u32[]{:S(2)}) copy-start(s32[4,26]{1,0:T(4,128)} %param.12) | copy-start | bytes 1252
  7.2 4.5 %copy-start.16 = (bf16[48,512]{1,0:T(8,128)(2,1)S(1)}, bf16[48,512]{1,0:T(8,128)(2,1)}, u32[]{:S(2)}) copy-start(bf16[48,512]{1,0:T(8,128)(2,1)} %param.15) | copy-start | bytes 147460
  7.2 4.5 %copy-start.17 = (bf16[48,512]{1,0:T(8,128)(2,1)S(1)}, bf16[48,512]{1,0:T(8,128)(2,1)}, u32[]{:S(2)}) copy-start(bf16[48,512]{1,0:T(8,128)(2,1)} %param.8) | copy-start | bytes 147460
  7.2 106.9 %reduce-scatter.13.cloned.1.call-start = ((), (), s32[]{:S(2)}) async-start(), calls=%async_computation.6 | async-start | bytes 5431296
  11.5 20.8 %copy-start = (bf16[512,3328]{0,1:T(8,128)(2,1)}, bf16[512,3328]{0,1:T(8,128)(2,1)S(1)}, u32[]{:S(2)}) copy-start(bf16[512,3328]{0,1:T(8,128)(2,1)S(1)} %copy.26) | copy-start | bytes 10223620
  32.3 3.5 copy-start.9
  32.3 164.4 %reduce-scatter.17.cloned.1.call-start = ((), (), s32[]{:S(2)}) async-start(), calls=%async_computation.8 | async-start | bytes 5431296
  39.7 4.4 %copy-start.20 = (s32[4,26]{1,0:T(4,128)S(1)}, s32[4,26]{1,0:T(4,128)}, u32[]{:S(2)}) copy-start(s32[4,26]{1,0:T(4,128)} %param.13) | copy-start | bytes 1252
  39.7 239.6 %reduce-scatter.15.cloned.1.call-start = ((), (), s32[]{:S(2)}) async-start(), calls=%async_computation.7 | async-start | bytes 5431296
  44.1 6.8 %copy-start.6 = (bf16[512,3328]{0,1:T(8,128)(2,1)}, bf16[512,3328]{0,1:T(8,128)(2,1)S(1)}, u32[]{:S(2)}) copy-start(bf16[512,3328]{0,1:T(8,128)(2,1)S(1)} %copy.28) | copy-start | bytes 10223620
  50.9 317.5 %all-gather.2.cloned.1.call-start = ((), (), s32[]{:S(2)}) async-start(), calls=%async_computation.4 | async-start | bytes 5431296 | tf_op jit(solution)/shard_map/all_gather | solution.py:81
  114.1 167.6 %copy-start.14 = (f32[24,3328]{1,0:T(8,128)S(1)}, f32[24,3328]{1,0:T(8,128)}, u32[]{:S(2)}) copy-start(f32[24,3328]{1,0:T(8,128)} %reduce-scatter.13.cloned.1.call-done) | copy-start | bytes 958468
  281.5 140.1 %reduce-scatter.11.cloned.1.call-start = ((), (), s32[]{:S(2)}) async-start(), calls=%async_computation.5 | async-start | bytes 1769472 | tf_op jit(solution)/shard_map/reduce_scatter | solution.py:93
  281.8 8.7 %collective-permute-start = (bf16[24,3328]{1,0:T(8,128)(2,1)S(1)}, bf16[24,3328]{1,0:T(8,128)(2,1)S(1)}, u32[]{:S(2)}, u32[]{:S(2)}) collective-permute-start(bf16[24,3328]{1,0:T(8,128)(2,1)S(1)} %get-tuple-element.6), channel_id=1, source_target_pairs={{0,8},{8,16},{16,24},{24,32},{32,40},{40,48},{48,56},{56,64},{64,7... | collective-permute-start | bytes 479240 | tf_op jit(solution)/shard_map/ppermute | solution.py:16
  283.0 7.5 %collective-permute-start.1 = (bf16[24,3328]{1,0:T(8,128)(2,1)S(1)}, bf16[24,3328]{1,0:T(8,128)(2,1)S(1)}, u32[]{:S(2)}, u32[]{:S(2)}) collective-permute-start(bf16[24,3328]{1,0:T(8,128)(2,1)S(1)} %get-tuple-element.6), channel_id=1, source_target_pairs={{0,120},{8,0},{16,8},{24,16},{32,24},{40,32},{48,40},{56,48},{64,5... | collective-permute-start | bytes 479240 | tf_op jit(solution)/shard_map/ppermute | solution.py:21
  287.2 77.6 %copy-start.5 = (bf16[26,128,4,128]{3,2,1,0:T(4,128)(2,1)S(1)}, bf16[26,128,4,128]{3,2,1,0:T(4,128)(2,1)}, u32[]{:S(2)}) copy-start(bf16[26,128,4,128]{3,2,1,0:T(4,128)(2,1)} %copy-done.4) | copy-start | bytes 10223620
  290.5 11.5 %collective-permute-start.2 = (bf16[24,3328]{1,0:T(8,128)(2,1)S(1)}, bf16[24,3328]{1,0:T(8,128)(2,1)S(1)}, u32[]{:S(2)}, u32[]{:S(2)}) collective-permute-start(bf16[24,3328]{1,0:T(8,128)(2,1)S(1)} %collective-permute-done), channel_id=1, source_target_pairs={{0,8},{8,16},{16,24},{24,32},{32,40},{40,48},{48,56},{56,64},{64,7... | collective-permute-start | bytes 479240 | tf_op jit(solution)/shard_map/ppermute | solution.py:16
  290.5 11.5 %collective-permute-start.3 = (bf16[24,3328]{1,0:T(8,128)(2,1)S(1)}, bf16[24,3328]{1,0:T(8,128)(2,1)S(1)}, u32[]{:S(2)}, u32[]{:S(2)}) collective-permute-start(bf16[24,3328]{1,0:T(8,128)(2,1)S(1)} %collective-permute-done.1), channel_id=1, source_target_pairs={{0,120},{8,0},{16,8},{24,16},{32,24},{40,32},{48,40},{56,48},{64,5... | collective-permute-start | bytes 479240 | tf_op jit(solution)/shard_map/ppermute | solution.py:21
  301.9 8.9 %collective-permute-start.4 = (bf16[24,3328]{1,0:T(8,128)(2,1)S(1)}, bf16[24,3328]{1,0:T(8,128)(2,1)S(1)}, u32[]{:S(2)}, u32[]{:S(2)}) collective-permute-start(bf16[24,3328]{1,0:T(8,128)(2,1)S(1)} %collective-permute-done.2), channel_id=1, source_target_pairs={{0,8},{8,16},{16,24},{24,32},{32,40},{40,48},{48,56},{56,64},{64,7... | collective-permute-start | bytes 479240 | tf_op jit(solution)/shard_map/ppermute | solution.py:16
  301.9 8.9 %collective-permute-start.5 = (bf16[24,3328]{1,0:T(8,128)(2,1)S(1)}, bf16[24,3328]{1,0:T(8,128)(2,1)S(1)}, u32[]{:S(2)}, u32[]{:S(2)}) collective-permute-start(bf16[24,3328]{1,0:T(8,128)(2,1)S(1)} %collective-permute-done.3), channel_id=1, source_target_pairs={{0,120},{8,0},{16,8},{24,16},{32,24},{40,32},{48,40},{56,48},{64,5... | collective-permute-start | bytes 479240 | tf_op jit(solution)/shard_map/ppermute | solution.py:21
  310.8 10.1 %collective-permute-start.6 = (bf16[24,3328]{1,0:T(8,128)(2,1)S(1)}, bf16[24,3328]{1,0:T(8,128)(2,1)S(1)}, u32[]{:S(2)}, u32[]{:S(2)}) collective-permute-start(bf16[24,3328]{1,0:T(8,128)(2,1)S(1)} %collective-permute-done.4), channel_id=1, source_target_pairs={{0,8},{8,16},{16,24},{24,32},{32,40},{40,48},{48,56},{56,64},{64,7... | collective-permute-start | bytes 479240 | tf_op jit(solution)/shard_map/ppermute | solution.py:16
  310.8 13.5 %collective-permute-start.7 = (bf16[24,3328]{1,0:T(8,128)(2,1)S(1)}, bf16[24,3328]{1,0:T(8,128)(2,1)S(1)}, u32[]{:S(2)}, u32[]{:S(2)}) collective-permute-start(bf16[24,3328]{1,0:T(8,128)(2,1)S(1)} %collective-permute-done.5), channel_id=1, source_target_pairs={{0,120},{8,0},{16,8},{24,16},{32,24},{40,32},{48,40},{56,48},{64,5... | collective-permute-start | bytes 479240 | tf_op jit(solution)/shard_map/ppermute | solution.py:21
  320.9 13.5 %collective-permute-start.8 = (bf16[24,3328]{1,0:T(8,128)(2,1)S(1)}, bf16[24,3328]{1,0:T(8,128)(2,1)S(1)}, u32[]{:S(2)}, u32[]{:S(2)}) collective-permute-start(bf16[24,3328]{1,0:T(8,128)(2,1)S(1)} %collective-permute-done.6), channel_id=1, source_target_pairs={{0,8},{8,16},{16,24},{24,32},{32,40},{40,48},{48,56},{56,64},{64,7... | collective-permute-start | bytes 479240 | tf_op jit(solution)/shard_map/ppermute | solution.py:16
  324.3 13.5 %collective-permute-start.9 = (bf16[24,3328]{1,0:T(8,128)(2,1)S(1)}, bf16[24,3328]{1,0:T(8,128)(2,1)S(1)}, u32[]{:S(2)}, u32[]{:S(2)}) collective-permute-start(bf16[24,3328]{1,0:T(8,128)(2,1)S(1)} %collective-permute-done.7), channel_id=1, source_target_pairs={{0,120},{8,0},{16,8},{24,16},{32,24},{40,32},{48,40},{56,48},{64,5... | collective-permute-start | bytes 479240 | tf_op jit(solution)/shard_map/ppermute | solution.py:21
  334.4 13.2 %collective-permute-start.10 = (bf16[24,3328]{1,0:T(8,128)(2,1)S(1)}, bf16[24,3328]{1,0:T(8,128)(2,1)S(1)}, u32[]{:S(2)}, u32[]{:S(2)}) collective-permute-start(bf16[24,3328]{1,0:T(8,128)(2,1)S(1)} %collective-permute-done.8), channel_id=1, source_target_pairs={{0,8},{8,16},{16,24},{24,32},{32,40},{40,48},{48,56},{56,64},{64,7... | collective-permute-start | bytes 479240 | tf_op jit(solution)/shard_map/ppermute | solution.py:16
  337.8 9.8 %collective-permute-start.11 = (bf16[24,3328]{1,0:T(8,128)(2,1)S(1)}, bf16[24,3328]{1,0:T(8,128)(2,1)S(1)}, u32[]{:S(2)}, u32[]{:S(2)}) collective-permute-start(bf16[24,3328]{1,0:T(8,128)(2,1)S(1)} %collective-permute-done.9), channel_id=1, source_target_pairs={{0,120},{8,0},{16,8},{24,16},{32,24},{40,32},{48,40},{56,48},{64,5... | collective-permute-start | bytes 479240 | tf_op jit(solution)/shard_map/ppermute | solution.py:21
  347.6 8.6 %collective-permute-start.12 = (bf16[24,3328]{1,0:T(8,128)(2,1)S(1)}, bf16[24,3328]{1,0:T(8,128)(2,1)S(1)}, u32[]{:S(2)}, u32[]{:S(2)}) collective-permute-start(bf16[24,3328]{1,0:T(8,128)(2,1)S(1)} %collective-permute-done.10), channel_id=1, source_target_pairs={{0,8},{8,16},{16,24},{24,32},{32,40},{40,48},{48,56},{56,64},{64,7... | collective-permute-start | bytes 479240 | tf_op jit(solution)/shard_map/ppermute | solution.py:16
  347.6 8.6 %collective-permute-start.13 = (bf16[24,3328]{1,0:T(8,128)(2,1)S(1)}, bf16[24,3328]{1,0:T(8,128)(2,1)S(1)}, u32[]{:S(2)}, u32[]{:S(2)}) collective-permute-start(bf16[24,3328]{1,0:T(8,128)(2,1)S(1)} %collective-permute-done.11), channel_id=1, source_target_pairs={{0,120},{8,0},{16,8},{24,16},{32,24},{40,32},{48,40},{56,48},{64,5... | collective-permute-start | bytes 479240 | tf_op jit(solution)/shard_map/ppermute | solution.py:21
  356.2 8.6 %collective-permute-start.14 = (bf16[24,3328]{1,0:T(8,128)(2,1)S(1)}, bf16[24,3328]{1,0:T(8,128)(2,1)S(1)}, u32[]{:S(2)}, u32[]{:S(2)}) collective-permute-start(bf16[24,3328]{1,0:T(8,128)(2,1)S(1)} %collective-permute-done.12), channel_id=1, source_target_pairs={{0,8},{8,16},{16,24},{24,32},{32,40},{40,48},{48,56},{56,64},{64,7... | collective-permute-start | bytes 479240 | tf_op jit(solution)/shard_map/ppermute | solution.py:16
  368.4 5.4 %copy-start.1 = (bf16[512,3328]{0,1:T(8,128)(2,1)S(1)}, bf16[512,3328]{0,1:T(8,128)(2,1)}, u32[]{:S(2)}) copy-start(bf16[512,3328]{0,1:T(8,128)(2,1)} %copy-done) | copy-start | bytes 10223620
  368.4 5.7 %copy-start.3 = (bf16[4,128,26,128]{1,0,3,2:T(4,128)(2,1)S(1)}, bf16[4,128,26,128]{1,0,3,2:T(4,128)(2,1)}, u32[]{:S(2)}) copy-start(bf16[4,128,26,128]{1,0,3,2:T(4,128)(2,1)} %copy-done.2) | copy-start | bytes 10223620
  368.4 7.2 %copy-start.12 = (bf16[384,6656]{1,0:T(8,128)(2,1)S(1)}, bf16[384,6656]{1,0:T(8,128)(2,1)}, u32[]{:S(2)}) copy-start(bf16[384,6656]{1,0:T(8,128)(2,1)} %all-gather.2.cloned.1.call-done) | copy-start | bytes 15335428
  (9 other events, 15.9 us)
Sparse Core Ops, SparseCore 0:
  32.4 81.6 reduce-scatter.12
  117.5 79.1 reduce-scatter.16
  200.1 79.2 reduce-scatter.14
  281.6 67.3 all-gather.1
  378.6 29.1 reduce-scatter.10
